TPU v7x, 32 devices: a whole 2x2x4 slice. The times are simulated.
32 devices in a mesh: grp: 2 (over x), tok: 4 (over z), head: 4 (over y, core).
Axes of the slice: x: 2, y: 2, z: 4, core: 2. Of those that a mesh axis runs over, the one named last changes fastest.
Arguments:
- views: bfloat16 [2, 2, 768, 1024], P('grp', None, 'tok'), may hold values from -6 to 6
- q_weight: bfloat16 [1024, 1024], P(None, 'head'), may hold values from -0.1875 to 0.1875
- k_weight: bfloat16 [1024, 1024], P(None, 'head'), may hold values from -0.1875 to 0.1875
- v_weight: bfloat16 [1024, 1024], P(None, 'head'), may hold values from -0.1875 to 0.1875
- rate_weight: bfloat16 [1024, 4], P(None, 'head'), may hold values from -0.1875 to 0.1875
- fast_in: float32 [4, 256, 1024], P('head', None, 'tok'), may hold values from -0.375 to 0.375
- fast_out: float32 [4, 512, 256], P('head', None, 'tok'), may hold values from -0.25 to 0.25
- out_gain: float32 [1024], P('head'), may hold values from 0.1 to 1.9
Outputs:
- rendered: bfloat16 [2, 2, 768, 1024], P('grp', None, 'tok', 'head')
All inputs are finite; a program needn't handle non-finite values.
Results may differ from a plain program's by a relative error of at most 0.013.
Values may be sent and summed in bfloat16 or wider, within the bound.
A program may use at most 64 MiB of HBM per device.

v0:
```python
import math
import jax
import jax.numpy as jnp
from jax import lax
from jax.sharding import PartitionSpec as P

norm_eps = 1e-06
out_eps = 1e-05
step_coef = 0.3
momentum_keep = 0.5


def spread(value, axis, source):
    kept = jnp.where(lax.axis_index(axis) == source, value, 0).astype(value.dtype)
    return lax.psum(kept, axis)


def rms_scale(values):
    return values * lax.rsqrt(jnp.mean(values * values, axis=-1, keepdims=True) + norm_eps)


def contract_rows(left, right):
    return lax.dot_general(
        left, right, (((0,), (0,)), ((), ())), preferred_element_type=jnp.float32
    )


def contract_cols(left, right):
    return lax.dot_general(
        left, right, (((1,), (1,)), ((), ())), preferred_element_type=jnp.float32
    )


def fast_apply(queries, copy_in, copy_out):
    hidden_units = copy_out.shape[0]
    pre_act = jnp.dot(queries, copy_in, preferred_element_type=jnp.float32)
    gate = pre_act[:, :hidden_units]
    upper = pre_act[:, hidden_units:]
    hidden = (gate * jax.nn.sigmoid(gate) * upper).astype(jnp.bfloat16)
    return jnp.dot(hidden, copy_out, preferred_element_type=jnp.float32)


def local(views, q_weight, k_weight, v_weight, rate_weight, fast_in, fast_out, out_gain):
    tok_count = lax.axis_size("tok")
    is_input = lax.axis_index("grp") == 0
    spans = views.shape[1]
    head_size = fast_in.shape[1]
    hidden_units = fast_out.shape[1]
    step_size = step_coef / math.sqrt(views.shape[2] * tok_count)
    width_all = head_size * lax.axis_size("head")
    whole_in, whole_out = (
        lax.all_gather(fast_in, "tok", axis=2, tiled=True),
        lax.all_gather(fast_out, "tok", axis=2, tiled=True),
    )
    whole_in = whole_in[0]
    whole_out = whole_out[0]
    copy_in = whole_in.astype(jnp.bfloat16)
    copy_out = whole_out.astype(jnp.bfloat16)
    state_in = fast_in[0]
    state_out = fast_out[0]
    base_in = jnp.mean(state_in * state_in, axis=0, keepdims=True)
    base_out = jnp.mean(state_out * state_out, axis=0, keepdims=True)
    moment_in = jnp.zeros_like(state_in)
    moment_out = jnp.zeros_like(state_out)

    def input_grads(inputs, given_in, given_out):
        keyed = rms_scale(jnp.dot(inputs, k_weight, preferred_element_type=jnp.float32)).astype(
            jnp.bfloat16
        )
        valued = jnp.dot(inputs, v_weight, preferred_element_type=jnp.float32)
        rates = jax.nn.softplus(jnp.dot(inputs, rate_weight, preferred_element_type=jnp.float32))
        upstream = (-(step_size * rates) * valued).astype(jnp.bfloat16)
        pre_act = jnp.dot(keyed, given_in, preferred_element_type=jnp.float32)
        gate = pre_act[:, :hidden_units]
        upper = pre_act[:, hidden_units:]
        sigma = jax.nn.sigmoid(gate)
        active = gate * sigma
        hidden = (active * upper).astype(jnp.bfloat16)
        grad_out = contract_rows(hidden, upstream)
        back = contract_cols(upstream, given_out)
        back_pre = jnp.concatenate(
            [back * upper * sigma * (1.0 + gate * (1.0 - sigma)), back * active], axis=1
        ).astype(jnp.bfloat16)
        grad_in = contract_rows(keyed, back_pre)
        return (grad_in, grad_out)

    def novel_grads(inputs, given_in, given_out):
        return (
            jnp.zeros((head_size, 2 * hidden_units), jnp.float32),
            jnp.zeros((hidden_units, head_size), jnp.float32),
        )

    outputs = []
    for span in range(spans):
        inputs = views[0, span]
        queries = rms_scale(jnp.dot(inputs, q_weight, preferred_element_type=jnp.float32)).astype(
            jnp.bfloat16
        )
        grads = lax.cond(is_input, input_grads, novel_grads, inputs, copy_in, copy_out)
        grad_in, grad_out = lax.psum_scatter(grads, "tok", scatter_dimension=1, tiled=True)
        moment_in = momentum_keep * moment_in + grad_in
        moment_out = momentum_keep * moment_out + grad_out
        trial_in = state_in - moment_in
        trial_out = state_out - moment_out
        mean_in = jnp.mean(trial_in * trial_in, axis=0, keepdims=True)
        mean_out = jnp.mean(trial_out * trial_out, axis=0, keepdims=True)
        state_in = trial_in * jnp.sqrt(base_in) * lax.rsqrt(mean_in + norm_eps)
        state_out = trial_out * jnp.sqrt(base_out) * lax.rsqrt(mean_out + norm_eps)
        part_in = state_in.astype(jnp.bfloat16)
        part_out = state_out.astype(jnp.bfloat16)
        copy_in, copy_out = (
            lax.all_gather(part_in, "tok", axis=1, tiled=True),
            lax.all_gather(part_out, "tok", axis=1, tiled=True),
        )
        copy_in, copy_out = (spread(copy_in, "grp", 0), spread(copy_out, "grp", 0))
        produced = fast_apply(queries, copy_in, copy_out)
        squares = lax.psum(jnp.sum(produced * produced, axis=1), "head")
        normed = produced * lax.rsqrt(squares / width_all + out_eps)[:, None] * out_gain
        outputs.append(normed.astype(jnp.bfloat16))
    return jnp.stack(outputs)[None]


def solution(mesh):
    placed = (
        P("grp", None, "tok", None),
        P(None, "head"),
        P(None, "head"),
        P(None, "head"),
        P(None, "head"),
        P("head", None, "tok"),
        P("head", None, "tok"),
        P("head"),
    )
    return jax.shard_map(
        local, mesh=mesh, in_specs=placed, out_specs=P("grp", None, "tok", "head"), check_vma=False
    )
```

profile of v0, /device:TPU:0, one launch (start us, length us, event | category | flops | bytes accessed | tf_op | source)
XLA Modules:
  0.0 281.3 jit_solution(5273160163596320403)
XLA Ops:
  6.5 1.2 slice_bitcast_fusion.1
  8.0 18.1 %all_gather.18 = bf16[1,512,256]{1,0,2:T(2,128)(2,1)} all-gather(bf16[1,512,64]{1,0,2:T(2,128)(2,1)S(1)} %copy.11), channel_id=1, replica_groups=mesh['grp'=2,'tok'=4,'head'=4] {'tok'}, dimensions={2}, use_global_device_ids=true | all-gather | bytes 327680 | tf_op jit(solution)/shard_map/all_gather | solution.py:53
  26.1 16.5 %all_gather.19 = bf16[1,256,1024]{2,1,0:T(8,128)(2,1)S(1)} all-gather(bf16[1,256,256]{2,1,0:T(8,128)(2,1)S(1)} %convert.16), channel_id=1, replica_groups=mesh['grp'=2,'tok'=4,'head'=4] {'tok'}, dimensions={2}, use_global_device_ids=true | all-gather | bytes 655360 | tf_op jit(solution)/shard_map/all_gather | solution.py:52
  42.6 7.0 %conditional.2 = (f32[256,1024]{1,0:T(8,128)S(1)}, f32[512,256]{1,0:T(8,128)}) conditional(s32[]{:T(128)} %convert_element_type.75, () %tuple.21, (bf16[192,1024]{1,0:T(8,128)(2,1)S(1)}, bf16[1024,256]{1,0:T(8,128)(2,1)S(1)}, bf16[1024,1]{0,1:T(2,128)(2,1)S(1)}, bf16[1024,256]{1,0:T(8,128)(2,1)S(1)}, bf16[1,512,256]{1,0,2:T(2,128)(2,1)}, ...), branch_computations={%region_1.0_spmd, %region_2.4_spmd} | conditional | flops 506758848 | bytes 14132096 | solution.py:99
  43.0 1.2 fusion.1
  44.8 0.7 copy-done.7
  45.5 0.5 copy.12
  46.0 1.4 multiply_convert_fusion.2
  47.4 0.4 fusion.4
  47.8 0.7 copy-done.11
  48.6 1.1 fusion.12
  49.7 2.4 copy.18
  52.2 0.7 reduce-scatter.9.cloned.1.call-update
  53.2 21.1 %reduce-scatter.13.cloned.1.call-done = f32[64,512]{1,0:T(8,128)} async-done(((f32[256,512]{1,0:T(8,128)}), f32[64,512]{1,0:T(8,128)}) %reduce-scatter.13.cloned.1.call-update) | async-done | bytes 131088
  74.3 1.0 copy.19
  75.6 15.5 %all_gather.21 = bf16[512,256]{0,1:T(8,128)(2,1)S(1)} all-gather(bf16[512,64]{0,1:T(8,128)(2,1)S(1)} %copy.14), channel_id=1, replica_groups=mesh['grp'=2,'tok'=4,'head'=4] {'tok'}, dimensions={1}, use_global_device_ids=true | all-gather | bytes 327680 | tf_op jit(solution)/shard_map/all_gather | solution.py:113
  91.2 0.7 broadcast_select_fusion.3
  91.9 11.3 %reduce-scatter.9.cloned.1.call-done = f32[256,256]{1,0:T(8,128)} async-done(((f32[256,1024]{1,0:T(8,128)}), f32[256,256]{1,0:T(8,128)}) %reduce-scatter.9.cloned.1.call-update) | async-done | bytes 262160 | tf_op jit(solution)/shard_map/reduce_scatter | solution.py:100
  103.2 1.1 fusion.34
  104.3 15.4 %all_gather.20 = bf16[256,1024]{1,0:T(8,128)(2,1)S(1)} all-gather(bf16[256,256]{1,0:T(8,128)(2,1)S(1)} %fusion.35), channel_id=1, replica_groups=mesh['grp'=2,'tok'=4,'head'=4] {'tok'}, dimensions={1}, use_global_device_ids=true | all-gather | bytes 655360 | tf_op jit(solution)/shard_map/all_gather | solution.py:112
  119.8 0.8 broadcast_select_fusion.1
  120.7 34.5 %all-reduce.8.cloned.1.call-done = (bf16[512,256]{0,1:T(8,128)(2,1)}, bf16[256,1024]{1,0:T(8,128)(2,1)}) async-done(((bf16[512,256]{0,1:T(8,128)(2,1)}, bf16[256,1024]{1,0:T(8,128)(2,1)}), (bf16[512,256]{0,1:T(8,128)(2,1)}, bf16[256,1024]{1,0:T(8,128)(2,1)})) %all-reduce.8.cloned.1.call-update) | async-done | bytes 786448 | tf_op jit(solution)/shard_map/psum | solution.py:15
  155.2 4.4 %conditional.3 = (f32[256,1024]{1,0:T(8,128)S(1)}, f32[512,256]{1,0:T(8,128)}) conditional(s32[]{:T(128)} %convert_element_type.75, () %tuple.23, (bf16[192,1024]{1,0:T(8,128)(2,1)S(1)}, bf16[1024,256]{1,0:T(8,128)(2,1)S(1)}, bf16[1024,1]{0,1:T(2,128)(2,1)S(1)}, bf16[1024,256]{1,0:T(8,128)(2,1)S(1)}, bf16[512,256]{0,1:T(8,128)(2,1)}, ...), branch_computations={%region_15.16_spmd, %region_16.18_spmd} | conditional | flops 506758848 | bytes 11772744 | solution.py:99
  155.6 0.7 copy-done.9
  157.1 0.7 copy-done.19
  158.0 0.4 fusion.19
  158.4 1.1 fusion.24
  159.5 2.4 copy.20
  162.0 0.5 reduce-scatter.11.cloned.1.call-update
  162.6 1.4 multiply_reduce_fusion.7
  164.0 0.4 multiply_reduce_fusion.9
  164.4 19.5 %reduce-scatter.15.cloned.1.call-done = f32[64,512]{1,0:T(8,128)} async-done(((f32[256,512]{1,0:T(8,128)}), f32[64,512]{1,0:T(8,128)}) %reduce-scatter.15.cloned.1.call-update) | async-done | bytes 131088
  184.0 1.0 copy.21
  185.2 15.6 %all_gather.23 = bf16[512,256]{0,1:T(8,128)(2,1)S(1)} all-gather(bf16[512,64]{0,1:T(8,128)(2,1)S(1)} %copy.16), channel_id=1, replica_groups=mesh['grp'=2,'tok'=4,'head'=4] {'tok'}, dimensions={1}, use_global_device_ids=true | all-gather | bytes 327680 | tf_op jit(solution)/shard_map/all_gather | solution.py:113
  200.9 0.7 broadcast_select_fusion.2
  201.6 11.1 %reduce-scatter.11.cloned.1.call-done = f32[256,256]{1,0:T(8,128)} async-done(((f32[256,1024]{1,0:T(8,128)}), f32[256,256]{1,0:T(8,128)}) %reduce-scatter.11.cloned.1.call-update) | async-done | bytes 262160 | tf_op jit(solution)/shard_map/reduce_scatter | solution.py:100
  212.7 1.0 multiply_reduce_fusion.3
  213.8 15.8 %all_gather.22 = bf16[256,1024]{1,0:T(8,128)(2,1)S(1)} all-gather(bf16[256,256]{1,0:T(8,128)(2,1)S(1)} %multiply_convert_fusion.15), channel_id=1, replica_groups=mesh['grp'=2,'tok'=4,'head'=4] {'tok'}, dimensions={1}, use_global_device_ids=true | all-gather | bytes 655360 | tf_op jit(solution)/shard_map/all_gather | solution.py:112
  229.5 0.8 broadcast_select_fusion
  230.4 1.0 copy-done.8
  231.7 0.6 copy-done.18
  232.4 0.4 multiply_reduce_fusion.8
  232.7 32.0 %all-reduce.6.cloned.1.call-done = (bf16[512,256]{0,1:T(8,128)(2,1)}, bf16[256,1024]{1,0:T(8,128)(2,1)}) async-done(((bf16[512,256]{0,1:T(8,128)(2,1)}, bf16[256,1024]{1,0:T(8,128)(2,1)}), (bf16[512,256]{0,1:T(8,128)(2,1)}, bf16[256,1024]{1,0:T(8,128)(2,1)})) %all-reduce.6.cloned.1.call-update) | async-done | bytes 786448 | tf_op jit(solution)/shard_map/psum | solution.py:15
  264.7 1.4 fusion.43
  266.1 0.4 multiply_reduce_fusion.6
  266.5 6.4 %all-reduce = (f32[192]{0:T(256)S(1)}, f32[192]{0:T(256)S(1)}) all-reduce(f32[192]{0:T(256)S(1)} %get-tuple-element.95, f32[192]{0:T(256)S(1)} %get-tuple-element.97), channel_id=1, replica_groups=mesh['grp'=2,'tok'=4,'head'=4] {'head'}, use_global_device_ids=true, to_apply=%region_25.26 | all-reduce | flops 384 | bytes 3072 | tf_op jit(solution)/shard_map/psum | solution.py:117
  272.9 0.7 copy-done.17
  273.7 0.7 maximum_bitcast_fusion
  (78 shorter events, 4.1 us)
Async XLA Ops:
  6.5 156.1 %copy-start = (bf16[1024,256]{1,0:T(8,128)(2,1)S(1)}, bf16[1024,256]{1,0:T(8,128)(2,1)}, u32[]{:S(2)}) copy-start(bf16[1024,256]{1,0:T(8,128)(2,1)} %param.13) | copy-start | bytes 1572868
  6.5 67.8 %reduce-scatter.13.cloned.1.call-start = ((), (), s32[]{:S(2)}) async-start(), calls=%async_computation.6 | async-start | bytes 655360
  6.5 1.2 copy-start.12
  7.9 18.2 %copy-start.1 = (f32[1,256,256]{2,1,0:T(8,128)S(1)}, f32[1,256,256]{2,1,0:T(8,128)}, u32[]{:S(2)}) copy-start(f32[1,256,256]{2,1,0:T(8,128)} %param.17) | copy-start | bytes 786436
  7.9 34.7 %copy-start.16 = (bf16[1024,1]{0,1:T(2,128)(2,1)S(1)}, bf16[1024,1]{0,1:T(2,128)(2,1)}, u32[]{:S(2)}) copy-start(bf16[1024,1]{0,1:T(2,128)(2,1)} %param.16) | copy-start | bytes 6148
  26.1 16.5 %copy-start.5 = (bf16[1024,256]{1,0:T(8,128)(2,1)S(1)}, bf16[1024,256]{1,0:T(8,128)(2,1)}, u32[]{:S(2)}) copy-start(bf16[1024,256]{1,0:T(8,128)(2,1)} %param.14) | copy-start | bytes 1572868
  26.1 16.5 %copy-start.6 = (bf16[1024,256]{1,0:T(8,128)(2,1)S(1)}, bf16[1024,256]{1,0:T(8,128)(2,1)}, u32[]{:S(2)}) copy-start(bf16[1024,256]{1,0:T(8,128)(2,1)} %param.15) | copy-start | bytes 1572868
  44.4 1.1 copy-start.7
  44.8 1.2 copy-start.14
  47.4 1.1 copy-start.11
  47.4 1.1 copy-start.15
  49.7 2.5 copy-start.2
  52.1 51.1 %reduce-scatter.9.cloned.1.call-start = ((), (), s32[]{:S(2)}) async-start(), calls=%async_computation.4 | async-start | bytes 1310720 | tf_op jit(solution)/shard_map/reduce_scatter | solution.py:100
  52.2 0.9 copy-start.13
  52.9 102.3 %all-reduce.8.cloned.1.call-start = ((), (), s32[]{:S(2)}) async-start(), calls=%async_computation.9 | async-start | bytes 1572864 | tf_op jit(solution)/shard_map/psum | solution.py:15
  103.2 1.1 copy-start.4
  120.6 63.3 %reduce-scatter.15.cloned.1.call-start = ((), (), s32[]{:S(2)}) async-start(), calls=%async_computation.7 | async-start | bytes 655360
  155.2 1.0 copy-start.9
  156.8 1.0 copy-start.19
  159.5 2.5 copy-start.3
  162.0 50.7 %reduce-scatter.11.cloned.1.call-start = ((), (), s32[]{:S(2)}) async-start(), calls=%async_computation.5 | async-start | bytes 1310720 | tf_op jit(solution)/shard_map/reduce_scatter | solution.py:100
  162.5 1.5 copy-start.10
  162.6 102.2 %all-reduce.6.cloned.1.call-start = ((), (), s32[]{:S(2)}) async-start(), calls=%async_computation.8 | async-start | bytes 1572864 | tf_op jit(solution)/shard_map/psum | solution.py:15
  230.4 1.0 copy-start.8
  231.4 0.9 copy-start.18
  264.7 1.4 copy-start.20
  272.9 0.7 copy-start.17
Sparse Core Ops, SparseCore 0:
  52.2 22.0 reduce-scatter.12
  76.6 26.4 reduce-scatter.8
  120.7 34.3 all-reduce.7
  162.1 21.8 reduce-scatter.14
  186.1 26.5 reduce-scatter.10
  230.5 34.1 all-reduce.5
where the time goes:
time: 282 us; the launch traced here: 281 us
  waiting for transfers between devices  131 us (46%)
  blocking collectives  103 us (37%)
  local copies, waits for them, and re-layouts  14.3 us (5%)
  between operations  13.7 us (5%)
  matrix products  12.1 us (4%)
  other arithmetic  6.49 us (2%)
    psum x2, waiting for transfers between devices, spread(): return lax.psum(kept, axis)  66.5 us
    unnamed x8, waiting for transfers between devices  42 us
    all_gather x2, blocking collectives, local(): lax.all_gather(part_in, 'tok', axis=1, tiled=True)  31.2 us
    all_gather x2, blocking collectives, local(): lax.all_gather(part_out, 'tok', axis=1, tiled=True)  31.2 us
    reduce_scatter x2, waiting for transfers between devices, local(): lax.psum_scatter(grads, 'tok', scatter_dimension=1, tiled=True)  22.4 us
    all_gather x1, blocking collectives, local(): lax.all_gather(fast_out, 'tok', axis=2, tiled=True)  18.1 us
    all_gather x1, blocking collectives, local(): lax.all_gather(fast_in, 'tok', axis=2, tiled=True)  16.5 us
    unnamed x36, local copies, waits for them, and re-layouts  9.64 us
  transfers between devices with their start and end apart: 6, of which 6 were waited for; matrix products, arithmetic and copies ran while one was open for 2% of the time, Pallas kernels for 0%

commit v1 on v0

--- a/solution.py
+++ b/solution.py
@@ -8,6 +8,28 @@
 out_eps = 1e-05
 step_coef = 0.3
 momentum_keep = 0.5
+
+
+def order_the_case(raw, row_axis):
+    built, everything, outcome_arr = (
+        jax.lax.axis_size(row_axis),
+        jax.lax.axis_index(row_axis),
+        raw.shape[2],
+    )
+    work_now, arr_out = (raw, 1)
+    while arr_out < built:
+        work_now = jnp.concatenate(
+            [
+                work_now,
+                jax.lax.ppermute(
+                    work_now, row_axis, [(to_i, (to_i - arr_out) % built) for to_i in range(built)]
+                ),
+            ],
+            axis=2,
+        )
+        arr_out = 2 * arr_out
+    k_now = jnp.roll(work_now, everything * outcome_arr, axis=2)
+    return k_now
 
 
 def spread(value, axis, source):
@@ -49,7 +71,7 @@
     step_size = step_coef / math.sqrt(views.shape[2] * tok_count)
     width_all = head_size * lax.axis_size("head")
     whole_in, whole_out = (
-        lax.all_gather(fast_in, "tok", axis=2, tiled=True),
+        order_the_case(fast_in, "tok"),
         lax.all_gather(fast_out, "tok", axis=2, tiled=True),
     )
     whole_in = whole_in[0]

time: 282 us -> 283 us (level)
  blocking collectives: 103 us -> 93.5 us
  starting transfers between devices: 0.2 us -> 6.81 us
  local copies, waits for them, and re-layouts: 14.3 us -> 18.1 us
    all_gather x1 -> x0, blocking collectives: 16.5 us -> none  [local(): lax.all_gather(fast_in, 'tok', axis=2, tiled=True)]
    ppermute x0 -> x2, starting transfers between devices: none -> 6.61 us  [order_the_case(): jax.lax.ppermute(work_now, row_axis, [(to_i, (to_i - arr_out) % built) fo...]
    all_gather x1, blocking collectives: 18.1 us -> 24.3 us  [local(): lax.all_gather(fast_out, 'tok', axis=2, tiled=True)]
    unnamed x36 -> x46, local copies, waits for them, and re-layouts: 9.64 us -> 13 us
  transfers between devices with their start and end apart: 6 -> 8, of which waited for: 6 -> 7; matrix products, arithmetic and copies ran while one was open for 2% -> 3% of each run, Pallas kernels for 0% -> 0%
where the time goes in v1:
time: 283 us
  waiting for transfers between devices  130 us (46%)
  blocking collectives  93.5 us (33%)
  local copies, waits for them, and re-layouts  18.1 us (6%)
  between operations  13.7 us (5%)
  matrix products  12.3 us (4%)
  other arithmetic  8.43 us (3%)
  starting transfers between devices  6.81 us (2%)
    psum x2, waiting for transfers between devices, spread(): return lax.psum(kept, axis)  65.1 us
    unnamed x8, waiting for transfers between devices  39.6 us
    all_gather x2, blocking collectives, local(): lax.all_gather(part_in, 'tok', axis=1, tiled=True)  31.7 us
    all_gather x2, blocking collectives, local(): lax.all_gather(part_out, 'tok', axis=1, tiled=True)  31.1 us
    all_gather x1, blocking collectives, local(): lax.all_gather(fast_out, 'tok', axis=2, tiled=True)  24.3 us
    reduce_scatter x2, waiting for transfers between devices, local(): lax.psum_scatter(grads, 'tok', scatter_dimension=1, tiled=True)  22.2 us
    unnamed x46, local copies, waits for them, and re-layouts  13 us
    ppermute x2, starting transfers between devices, order_the_case(): jax.lax.ppermute(work_now, row_axis, [(to_i, (to_i - arr_out) % built) fo...  6.61 us
  transfers between devices with their start and end apart: 8, of which 7 were waited for; matrix products, arithmetic and copies ran while one was open for 3% of the time, Pallas kernels for 0%

profile of v1, /device:TPU:0, one launch (start us, length us, event | category | flops | bytes accessed | tf_op | source)
XLA Modules:
  0.0 282.7 jit_solution(2551020210425110188)
XLA Ops:
  6.5 1.8 fusion.52
  8.4 5.1 %collective-permute-start = (bf16[1,256,256]{2,1,0:T(8,128)(2,1)S(1)}, bf16[1,256,256]{2,1,0:T(8,128)(2,1)S(1)}, u32[]{:S(2)}, u32[]{:S(2)}) collective-permute-start(bf16[1,256,256]{2,1,0:T(8,128)(2,1)S(1)} %get-tuple-element.220), channel_id=1, source_target_pairs={{0,12},{4,0},{8,4},{12,8},{1,13},{5,1},{9,5},{13,9},{2,14},{6,2},{... | collective-permute-start | bytes 393224 | tf_op jit(solution)/shard_map/ppermute | solution.py:24
  13.5 2.8 collective-permute-done
  16.3 1.5 collective-permute-start.1
  18.0 24.3 %all_gather.15 = bf16[1,512,256]{1,0,2:T(2,128)(2,1)} all-gather(bf16[1,512,64]{1,0,2:T(2,128)(2,1)S(1)} %copy.11), channel_id=1, replica_groups=mesh['grp'=2,'tok'=4,'head'=4] {'tok'}, dimensions={2}, use_global_device_ids=true | all-gather | bytes 327680 | tf_op jit(solution)/shard_map/all_gather | solution.py:75
  42.3 0.7 constant_dynamic-update-slice_fusion.4
  43.0 0.8 constant_dynamic-update-slice_fusion.3
  43.8 0.7 constant_dynamic-update-slice_fusion.2
  44.5 0.7 constant_dynamic-update-slice_fusion.1
  45.2 0.7 constant_dynamic-update-slice_fusion
  45.9 8.0 %conditional.2 = (f32[256,1024]{1,0:T(8,128)S(1)}, f32[512,256]{1,0:T(8,128)}) conditional(s32[]{:T(128)} %convert_element_type.93, () %tuple.32, (bf16[192,1024]{1,0:T(8,128)(2,1)S(1)}, bf16[1024,256]{1,0:T(8,128)(2,1)S(1)}, bf16[1024,1]{0,1:T(2,128)(2,1)S(1)}, bf16[1024,256]{1,0:T(8,128)(2,1)S(1)}, bf16[1,512,256]{1,0,2:T(2,128)(2,1)}, ...), branch_computations={%region_1.2_spmd, %region_2.4_spmd.clone} | conditional | flops 506758848 | bytes 18326844 | solution.py:121
  46.3 0.8 copy-done.13
  47.2 1.3 fusion.15
  49.0 0.7 copy-done.7
  50.2 1.4 multiply_convert_fusion.9
  52.1 0.7 copy-done.12
  52.8 1.1 fusion.25
  53.9 2.4 copy.18
  56.5 0.7 reduce-scatter.9.cloned.1.call-update
  57.5 18.8 %reduce-scatter.13.cloned.1.call-done = f32[64,512]{1,0:T(8,128)} async-done(((f32[256,512]{1,0:T(8,128)}), f32[64,512]{1,0:T(8,128)}) %reduce-scatter.13.cloned.1.call-update) | async-done | bytes 131088
  76.3 1.0 copy.19
  78.1 15.5 %all_gather.17 = bf16[512,256]{0,1:T(8,128)(2,1)S(1)} all-gather(bf16[512,64]{0,1:T(8,128)(2,1)S(1)} %copy.14), channel_id=1, replica_groups=mesh['grp'=2,'tok'=4,'head'=4] {'tok'}, dimensions={1}, use_global_device_ids=true | all-gather | bytes 327680 | tf_op jit(solution)/shard_map/all_gather | solution.py:135
  93.6 0.7 broadcast_select_fusion.3
  94.4 11.0 %reduce-scatter.9.cloned.1.call-done = f32[256,256]{1,0:T(8,128)} async-done(((f32[256,1024]{1,0:T(8,128)}), f32[256,256]{1,0:T(8,128)}) %reduce-scatter.9.cloned.1.call-update) | async-done | bytes 262160 | tf_op jit(solution)/shard_map/reduce_scatter | solution.py:122
  105.4 1.1 fusion.35
  106.6 15.9 %all_gather.16 = bf16[256,1024]{1,0:T(8,128)(2,1)S(1)} all-gather(bf16[256,256]{1,0:T(8,128)(2,1)S(1)} %fusion.36), channel_id=1, replica_groups=mesh['grp'=2,'tok'=4,'head'=4] {'tok'}, dimensions={1}, use_global_device_ids=true | all-gather | bytes 655360 | tf_op jit(solution)/shard_map/all_gather | solution.py:134
  122.5 0.8 broadcast_select_fusion.1
  123.4 33.3 %all-reduce.8.cloned.1.call-done = (bf16[512,256]{0,1:T(8,128)(2,1)}, bf16[256,1024]{1,0:T(8,128)(2,1)}) async-done(((bf16[512,256]{0,1:T(8,128)(2,1)}, bf16[256,1024]{1,0:T(8,128)(2,1)}), (bf16[512,256]{0,1:T(8,128)(2,1)}, bf16[256,1024]{1,0:T(8,128)(2,1)})) %all-reduce.8.cloned.1.call-update) | async-done | bytes 786448 | tf_op jit(solution)/shard_map/psum | solution.py:37
  156.7 4.4 %conditional.3 = (f32[256,1024]{1,0:T(8,128)S(1)}, f32[512,256]{1,0:T(8,128)}) conditional(s32[]{:T(128)} %convert_element_type.93, () %tuple.34, (bf16[192,1024]{1,0:T(8,128)(2,1)S(1)}, bf16[1024,256]{1,0:T(8,128)(2,1)S(1)}, bf16[1024,1]{0,1:T(2,128)(2,1)S(1)}, bf16[1024,256]{1,0:T(8,128)(2,1)S(1)}, bf16[512,256]{0,1:T(8,128)(2,1)}, ...), branch_computations={%region_15.16_spmd, %region_16.18_spmd} | conditional | flops 506758848 | bytes 11772744 | solution.py:121
  157.1 0.7 copy-done.9
  158.6 0.7 copy-done.23
  160.0 1.1 fusion.6
  161.1 2.4 copy.20
  164.2 1.4 multiply_reduce_fusion.7
  166.0 19.5 %reduce-scatter.15.cloned.1.call-done = f32[64,512]{1,0:T(8,128)} async-done(((f32[256,512]{1,0:T(8,128)}), f32[64,512]{1,0:T(8,128)}) %reduce-scatter.15.cloned.1.call-update) | async-done | bytes 131088
  185.5 1.0 copy.21
  186.8 15.5 %all_gather.19 = bf16[512,256]{0,1:T(8,128)(2,1)S(1)} all-gather(bf16[512,64]{0,1:T(8,128)(2,1)S(1)} %copy.16), channel_id=1, replica_groups=mesh['grp'=2,'tok'=4,'head'=4] {'tok'}, dimensions={1}, use_global_device_ids=true | all-gather | bytes 327680 | tf_op jit(solution)/shard_map/all_gather | solution.py:135
  202.3 0.7 broadcast_select_fusion.2
  203.1 11.2 %reduce-scatter.11.cloned.1.call-done = f32[256,256]{1,0:T(8,128)} async-done(((f32[256,1024]{1,0:T(8,128)}), f32[256,256]{1,0:T(8,128)}) %reduce-scatter.11.cloned.1.call-update) | async-done | bytes 262160 | tf_op jit(solution)/shard_map/reduce_scatter | solution.py:122
  214.3 1.0 multiply_reduce_fusion.3
  215.4 15.8 %all_gather.18 = bf16[256,1024]{1,0:T(8,128)(2,1)S(1)} all-gather(bf16[256,256]{1,0:T(8,128)(2,1)S(1)} %multiply_convert_fusion.15), channel_id=1, replica_groups=mesh['grp'=2,'tok'=4,'head'=4] {'tok'}, dimensions={1}, use_global_device_ids=true | all-gather | bytes 655360 | tf_op jit(solution)/shard_map/all_gather | solution.py:134
  231.1 0.8 broadcast_select_fusion
  232.0 1.0 copy-done.8
  234.3 31.8 %all-reduce.6.cloned.1.call-done = (bf16[512,256]{0,1:T(8,128)(2,1)}, bf16[256,1024]{1,0:T(8,128)(2,1)}) async-done(((bf16[512,256]{0,1:T(8,128)(2,1)}, bf16[256,1024]{1,0:T(8,128)(2,1)}), (bf16[512,256]{0,1:T(8,128)(2,1)}, bf16[256,1024]{1,0:T(8,128)(2,1)})) %all-reduce.6.cloned.1.call-update) | async-done | bytes 786448 | tf_op jit(solution)/shard_map/psum | solution.py:37
  266.1 1.4 fusion.44
  267.9 6.4 %all-reduce = (f32[192]{0:T(256)S(1)}, f32[192]{0:T(256)S(1)}) all-reduce(f32[192]{0:T(256)S(1)} %get-tuple-element.228, f32[192]{0:T(256)S(1)} %get-tuple-element.230), channel_id=1, replica_groups=mesh['grp'=2,'tok'=4,'head'=4] {'head'}, use_global_device_ids=true, to_apply=%region_25.26 | all-reduce | flops 384 | bytes 3072 | tf_op jit(solution)/shard_map/psum | solution.py:139
  274.3 0.7 copy-done.21
  275.2 0.7 maximum_bitcast_fusion
  (95 shorter events, 8.2 us)
Async XLA Ops:
  6.5 157.6 %copy-start = (bf16[1024,256]{1,0:T(8,128)(2,1)S(1)}, bf16[1024,256]{1,0:T(8,128)(2,1)}, u32[]{:S(2)}) copy-start(bf16[1024,256]{1,0:T(8,128)(2,1)} %param.13) | copy-start | bytes 1572868
  6.5 9.7 %copy-start.1 = (f32[1,256,256]{2,1,0:T(8,128)S(1)}, f32[1,256,256]{2,1,0:T(8,128)}, u32[]{:S(2)}) copy-start(f32[1,256,256]{2,1,0:T(8,128)} %param.17) | copy-start | bytes 786436
  6.5 11.3 %copy-start.10 = (bf16[1,2,192,1024]{3,2,1,0:T(8,128)(2,1)S(1)}, bf16[1,2,192,1024]{3,2,1,0:T(8,128)(2,1)}, u32[]{:S(2)}) copy-start(bf16[1,2,192,1024]{3,2,1,0:T(8,128)(2,1)} %param.12) | copy-start | bytes 2359300
  6.5 69.7 %reduce-scatter.13.cloned.1.call-start = ((), (), s32[]{:S(2)}) async-start(), calls=%async_computation.6 | async-start | bytes 655360
  8.4 7.8 %collective-permute-start = (bf16[1,256,256]{2,1,0:T(8,128)(2,1)S(1)}, bf16[1,256,256]{2,1,0:T(8,128)(2,1)S(1)}, u32[]{:S(2)}, u32[]{:S(2)}) collective-permute-start(bf16[1,256,256]{2,1,0:T(8,128)(2,1)S(1)} %get-tuple-element.220), channel_id=1, source_target_pairs={{0,12},{4,0},{8,4},{12,8},{1,13},{5,1},{9,5},{13,9},{2,14},{6,2},{... | collective-permute-start | bytes 393224 | tf_op jit(solution)/shard_map/ppermute | solution.py:24
  16.3 1.6 copy-start.14
  16.3 26.7 %collective-permute-start.1 = (bf16[1,256,512]{2,1,0:T(8,128)(2,1)S(1)}, bf16[1,256,512]{2,1,0:T(8,128)(2,1)S(1)}, u32[]{:S(2)}, u32[]{:S(2)}) collective-permute-start(bf16[1,256,512]{2,1,0:T(8,128)(2,1)S(1)} %pad_maximum_fusion), channel_id=1, source_target_pairs={{0,8},{4,12},{8,0},{12,4},{1,9},{5,13},{9,1},{13,5},{2,10},{6,14},... | collective-permute-start | bytes 786440 | tf_op jit(solution)/shard_map/ppermute | solution.py:24
  43.8 2.1 copy-start.6
  44.5 1.4 copy-start.5
  45.2 0.7 copy-start.18
  45.9 1.2 copy-start.13
  48.7 1.0 copy-start.7
  49.0 1.2 copy-start.16
  51.7 1.1 copy-start.12
  51.7 1.1 copy-start.17
  53.9 2.5 copy-start.2
  56.4 49.0 %reduce-scatter.9.cloned.1.call-start = ((), (), s32[]{:S(2)}) async-start(), calls=%async_computation.4 | async-start | bytes 1310720 | tf_op jit(solution)/shard_map/reduce_scatter | solution.py:122
  56.4 0.9 copy-start.15
  57.1 99.6 %all-reduce.8.cloned.1.call-start = ((), (), s32[]{:S(2)}) async-start(), calls=%async_computation.9 | async-start | bytes 1572864 | tf_op jit(solution)/shard_map/psum | solution.py:37
  77.4 0.5 copy-start.19
  105.4 1.1 copy-start.4
  123.4 62.1 %reduce-scatter.15.cloned.1.call-start = ((), (), s32[]{:S(2)}) async-start(), calls=%async_computation.7 | async-start | bytes 655360
  156.7 1.0 copy-start.9
  158.3 1.0 copy-start.23
  161.1 2.5 copy-start.3
  163.5 50.8 %reduce-scatter.11.cloned.1.call-start = ((), (), s32[]{:S(2)}) async-start(), calls=%async_computation.5 | async-start | bytes 1310720 | tf_op jit(solution)/shard_map/reduce_scatter | solution.py:122
  164.1 1.5 copy-start.11
  164.1 102.0 %all-reduce.6.cloned.1.call-start = ((), (), s32[]{:S(2)}) async-start(), calls=%async_computation.8 | async-start | bytes 1572864 | tf_op jit(solution)/shard_map/psum | solution.py:37
  185.5 1.1 copy-start.20
  232.0 1.0 copy-start.8
  233.0 0.9 copy-start.22
  266.1 1.4 copy-start.24
  274.3 0.7 copy-start.21
Sparse Core Ops, SparseCore 0:
  56.5 19.7 reduce-scatter.12
  78.6 26.7 reduce-scatter.8
  123.5 33.1 all-reduce.7
  163.6 21.8 reduce-scatter.14
  187.6 26.6 reduce-scatter.10
  232.1 33.9 all-reduce.5
